TPU v7x, 256 devices: a whole 4x4x8 slice. The times are simulated.
256 devices in a mesh: rows: 64 (over z_hi, x, y), rank: 4 (over z_lo, core).
Axes of the slice: x: 4, y: 4, z: 8 (z_hi: 4, z_lo: 2; z = z_hi * 2 + z_lo), core: 2. Of those that a mesh axis runs over, the one named last changes fastest.
Arguments:
- control: bfloat16 [1024, 64, 8, 128], P('rank', 'rows'), may hold values from -6 to 6
- observe: bfloat16 [1024, 8, 128, 64], P('rank', None, 'rows'), may hold values from -6 to 6
- capacity: float32 [64, 8, 128], P('rows'), may hold values from 0.5 to 2
- conduct: float32 [64, 8, 128], P('rows'), may hold values from 0.5 to 2
Outputs:
- left_basis: bfloat16 [1024, 64, 8, 128], P('rank', 'rows')
- stiff_basis: bfloat16 [1024, 64, 8, 128], P('rank', 'rows')
All inputs are finite; a program needn't handle non-finite values.
Results may differ from a plain program's by a relative error of at most 0.0067.
Values may be sent and summed in bfloat16 or wider, within the bound.
No kernel may reach another device: no remote copies, remote signals or barrier semaphores. Data moves between devices by JAX's collectives and lax.ppermute only.
A program may use at most 128 MiB of HBM per device.

v0:
```python
import jax
import jax.numpy as jnp
from jax import lax
from jax.experimental import pallas as pl
from jax.experimental.pallas import tpu as pltpu
from jax.sharding import Mesh
from jax.sharding import PartitionSpec as P


ONE_SIXTH = 1.0 / 6.0
F32 = jnp.float32
BF16 = jnp.bfloat16
ROWS = ("zh", "x", "y")
RANK = ("zl", "core")
COLS = 1024
OWN = 256
SIDE = 128
TILES = COLS // SIDE
LANES = 128
GROUP = 8


def neighbours(x):
    count = lax.axis_size(ROWS)
    up = [(i, i + 1) for i in range(count - 1)]
    down = [(j, i) for i, j in up]
    before = lax.ppermute(x, ROWS, up)
    after = lax.ppermute(x, ROWS, down)
    return before, after


def spread(padded, along_dim, side_weight, centre):
    length = padded.shape[along_dim] - 2
    before = lax.slice_in_dim(padded, 0, length, axis=along_dim)
    middle = lax.slice_in_dim(padded, 1, length + 1, axis=along_dim)
    beyond = lax.slice_in_dim(padded, 2, length + 2, axis=along_dim)
    return side_weight * (before + beyond) + centre * middle


def apply_line(values, along_dim, side_weight, centre):
    widths = [(0, 0)] * values.ndim
    widths[along_dim] = (1, 1)
    return spread(jnp.pad(values, widths), along_dim, side_weight, centre)


def mass_apply(padded):
    result = spread(padded, 1, ONE_SIXTH, 4.0 * ONE_SIXTH)
    result = apply_line(result, 2, ONE_SIXTH, 4.0 * ONE_SIXTH)
    return apply_line(result, 3, ONE_SIXTH, 4.0 * ONE_SIXTH)


def stiff_apply(padded):
    mass_x = spread(padded, 1, ONE_SIXTH, 4.0 * ONE_SIXTH)
    stiff_x = spread(padded, 1, -1.0, 2.0)
    first = apply_line(
        apply_line(stiff_x, 3, ONE_SIXTH, 4.0 * ONE_SIXTH), 2, ONE_SIXTH, 4.0 * ONE_SIXTH
    )
    second = apply_line(apply_line(mass_x, 3, -1.0, 2.0), 2, ONE_SIXTH, 4.0 * ONE_SIXTH)
    third = apply_line(apply_line(mass_x, 3, ONE_SIXTH, 4.0 * ONE_SIXTH), 2, -1.0, 2.0)
    return first + second + third


def halves(x):
    high = x.astype(BF16)
    return high, (x - high.astype(F32)).astype(BF16)


def product(a, b, a_dim=1, b_dim=0):
    dims = (((a_dim,), (b_dim,)), ((), ()))

    def one(p, q):
        return lax.dot_general(p, q, dims, preferred_element_type=F32)

    return one(a[0], b[0]) + (one(a[0], b[1]) + one(a[1], b[0]))


def factor_block(block):
    lane = lax.broadcasted_iota(jnp.int32, (GROUP, SIDE), 1)
    sub = lax.broadcasted_iota(jnp.int32, (GROUP, SIDE), 0)
    count = SIDE // GROUP

    def wide(row):
        return jnp.broadcast_to(row, (GROUP, SIDE))

    def columns(tile, base):
        return [wide(tile[:, base + t : base + t + 1]) for t in range(GROUP)]

    rows = [block[GROUP * v : GROUP * (v + 1), :] for v in range(count)]
    own = columns(rows[0], 0)
    out = []
    for g in range(count):
        base = g * GROUP
        inside = (lane >= base) & (lane < base + GROUP)
        body = jnp.where(inside, 0.0, rows[g])
        pivots = jnp.ones((GROUP, SIDE), F32)
        uppers, inverses, pivot_rows = [], [], []
        for s in range(GROUP):
            pivot = wide(own[s][s : s + 1, :])
            inverse = 1.0 / pivot
            upper = {t: wide(own[t][s : s + 1, :]) for t in range(s + 1, GROUP)}
            taken = jnp.where(sub > s, own[s] * inverse, 0.0)
            pivot_row = jnp.where(lane == base + s, 1.0, wide(body[s : s + 1, :]))
            for t in range(s + 1, GROUP):
                own[t] = own[t] - taken * upper[t]
            body = body - taken * pivot_row
            pivots = jnp.where(sub == s, pivot, pivots)
            uppers.append(upper)
            inverses.append(inverse)
            pivot_rows.append(pivot_row)
        for v in range(g + 1, count):
            cols = columns(rows[v], base)
            new = jnp.where(inside, 0.0, rows[v])
            ahead = columns(rows[v], base + GROUP) if v == g + 1 else []
            for s in range(GROUP):
                taken = cols[s] * inverses[s]
                ahead = [a - taken * wide(cols[s][t : t + 1, :]) for t, a in enumerate(ahead)]
                for t in range(s + 1, GROUP):
                    cols[t] = cols[t] - taken * uppers[s][t]
                new = new - taken * pivot_rows[s]
            rows[v] = new
            own = ahead or own
        low = jnp.where(lane == sub + base, 1.0, jnp.where(lane < base + GROUP, body, 0.0))
        scale = lax.rsqrt(pivots)
        scale = scale * (1.5 - 0.5 * pivots * scale * scale)
        out.append(low * scale)
    return jnp.concatenate(out, axis=0)


def factor_kernel(where, left, right, left_other, right_other, inv_out, proj_out, high, low, m, r_high, r_low):
    core = where[1]
    strip = OWN // 4

    def load(r, squares):
        inner = pl.ds(pl.multiple_of(r * strip, strip), strip)
        for half, pair in enumerate(((left, left_other), (right, right_other))):
            for chip in range(2):
                for other, source in enumerate(pair):
                    block = chip * 2 + (core if other == 0 else 1 - core)
                    lanes = pl.ds(pl.multiple_of(block * OWN + half * LANES, LANES), LANES)
                    x = source[chip, inner, :]
                    for at in range(0, strip, GROUP):
                        squares = squares + x[at : at + GROUP] * x[at : at + GROUP]
                    upper, lower = halves(x)
                    target = (block ^ (r // 4)) * OWN + (r % 4) * strip
                    rows = pl.ds(pl.multiple_of(target, strip), strip)
                    high[rows, lanes] = upper
                    low[rows, lanes] = lower
        return squares

    squares = lax.fori_loop(0, COLS // strip, load, jnp.zeros((GROUP, LANES), F32))
    total = jnp.sum(jnp.sum(squares, axis=0, keepdims=True), axis=1, keepdims=True)
    level = total / COLS + 1e-6
    scale = 1.0 / level
    eye = (lax.broadcasted_iota(jnp.int32, (SIDE, SIDE), 0) == lax.broadcasted_iota(jnp.int32, (SIDE, SIDE), 1)).astype(F32)

    def gram(a, carry):
        left_rows = pl.ds(pl.multiple_of(a * OWN, OWN), OWN)

        def one(b, inner):
            right_rows = pl.ds(pl.multiple_of(b * OWN, OWN), OWN)
            pair = product(
                (high[left_rows, :], low[left_rows, :]),
                (high[right_rows, :], low[right_rows, :]),
                1,
                1,
            )
            m[left_rows, right_rows] = pair * scale
            return inner

        return lax.fori_loop(a, COLS // OWN, one, carry)

    lax.fori_loop(0, COLS // OWN, gram, 0)

    def step(k, carry):
        block = pl.ds(pl.multiple_of(k * SIDE, SIDE), SIDE)
        x = factor_block(m[block, block] + eye)
        m[block, block] = eye
        r = product(halves(x), halves(m[block, :]))
        m[block, :] = r
        upper, lower = halves(r)
        r_high[...] = upper
        r_low[...] = lower

        def update(i, inner):
            rows = pl.ds(pl.multiple_of(i * SIDE, SIDE), SIDE)
            m[rows, block] = jnp.zeros((SIDE, SIDE), F32)
            mine = (r_high[:, rows], r_low[:, rows])
            m[rows, :] = m[rows, :] - product(mine, (r_high[...], r_low[...]), 0, 0)
            return inner

        lax.fori_loop(k + 1, TILES, update, 0)
        return carry

    lax.fori_loop(0, TILES, step, 0)
    first = pl.multiple_of(where[0] * OWN, OWN)
    row = lax.broadcasted_iota(jnp.int32, (OWN, OWN), 0)
    column = lax.broadcasted_iota(jnp.int32, (OWN, OWN), 1)
    own = []
    for block in range(4):
        part = m[pl.ds(first, OWN), block * OWN : (block + 1) * OWN]
        own.append(jnp.where(column + block * OWN <= row + first, part, 0.0))
    own = halves(jnp.concatenate(own, axis=1))
    shrink = lax.rsqrt(level)

    def project(turn, carry):
        block = where[0] ^ turn
        lanes = pl.ds(pl.multiple_of(block * OWN, OWN), OWN)
        out = pl.ds(pl.multiple_of(turn * OWN, OWN), OWN)
        part = m[pl.ds(first, OWN), lanes]
        part = jnp.where(column + block * OWN <= row + first, part, 0.0)
        inv_out[:, out] = part.astype(BF16)
        proj_out[:, out] = (product(own, (high[:, lanes], low[:, lanes])) * shrink).astype(BF16)
        return carry

    lax.fori_loop(0, 4, project, 0)


def factor(where, left, right, left_other, right_other):
    vmem = pl.BlockSpec(memory_space=pltpu.VMEM)
    return pl.pallas_call(
        factor_kernel,
        out_shape=(jax.ShapeDtypeStruct((OWN, COLS), BF16),) * 2,
        in_specs=[pl.BlockSpec(memory_space=pltpu.SMEM)] + [vmem] * 4,
        out_specs=[vmem] * 2,
        scratch_shapes=[
            pltpu.VMEM((COLS, COLS), BF16),
            pltpu.VMEM((COLS, COLS), BF16),
            pltpu.VMEM((COLS, COLS), F32),
            pltpu.VMEM((SIDE, COLS), BF16),
            pltpu.VMEM((SIDE, COLS), BF16),
        ],
        compiler_params=pltpu.CompilerParams(vmem_limit_bytes=20 * 2**20),
    )(where, left, right, left_other, right_other)


def gather_four(x, axis, dim):
    here = lax.axis_index(axis)
    shape = list(x.shape)
    shape[dim] = 4
    full = lax.dynamic_update_slice_in_dim(jnp.zeros(shape, x.dtype), x, here, dim)
    for step in (1, 2, 3):
        moved = lax.ppermute(x, axis, [(d, (d + step) % 4) for d in range(4)])
        full = lax.dynamic_update_slice_in_dim(full, moved, (here - step) % 4, dim)
    return full


def turned(x):
    moved = [lax.ppermute(x, RANK, [(d, d ^ step) for d in range(4)]) for step in (1, 2, 3)]
    return jnp.concatenate([x] + moved, axis=0)


SWAP = [(0, 1), (1, 0)]


def relayed(x, across, axis):
    near = lax.ppermute(x, "core", SWAP)
    return jnp.concatenate([x, near, across, lax.ppermute(across, "core", SWAP)], axis=axis)


def replane(observe):
    columns, depth, own, _ = observe.shape
    planes = jnp.transpose(observe.reshape(columns, depth, own, 4, 16), (4, 3, 2, 1, 0))
    planes = lax.all_to_all(planes, ("x", "y"), split_axis=0, concat_axis=0, tiled=True)
    here = lax.axis_index("zh")
    held = jnp.zeros((4, 16, own, depth, columns), observe.dtype)
    held = lax.dynamic_update_slice_in_dim(
        held, lax.dynamic_index_in_dim(planes, here, 1, False)[None], here, 0
    )
    came = []
    for step in (1, 2, 3):
        leaving = lax.dynamic_index_in_dim(planes, (here + step) % 4, 1, False)
        came.append(lax.ppermute(leaving, "zh", [(d, (d + step) % 4) for d in range(4)]))
    for step in (1, 2, 3):
        held = lax.dynamic_update_slice_in_dim(held, came[step - 1][None], (here - step) % 4, 0)
    return jnp.transpose(held, (3, 0, 1, 2, 4)).reshape(depth * 64 * own, columns)


def rounded(x):
    return lax.reduce_precision(x, 8, 7).astype(BF16)


def project(control, observe, capacity, conduct):
    col_rows = control.shape[0]
    local_cells = control.shape[1] * control.shape[2] * control.shape[3]
    before, after = neighbours(control)
    coefficients = jnp.stack([capacity, conduct])
    coefficients_before, coefficients_after = neighbours(coefficients)
    relaid = replane(observe)
    capacities, conducts = jnp.concatenate(
        [coefficients_before, coefficients, coefficients_after], axis=1
    )
    control_wide = jnp.concatenate([before, control, after], axis=1)
    widened = rounded(capacities * control_wide.astype(F32))
    applied = (capacity * mass_apply(widened.astype(F32))).astype(BF16)
    applied_flat = applied.reshape(col_rows, local_cells)
    applied_all = relayed(applied_flat, lax.ppermute(applied_flat, "zl", SWAP), 0)
    part = jnp.dot(applied_all, relaid, preferred_element_type=F32)
    relaid, part = lax.optimization_barrier((relaid, part))
    across = lax.ppermute(relaid, "zl", SWAP)
    pieces = lax.all_to_all(part, ("x", "y"), split_axis=0, concat_axis=0, tiled=True)
    pieces, across = lax.optimization_barrier((pieces, across))
    relaid_all = relayed(relaid, across, 1)
    chunk = jnp.sum(pieces.reshape(16, COLS // 16, OWN), axis=0)
    spread_out = jnp.broadcast_to(chunk, (8, COLS // 16, OWN))
    pair = lax.all_to_all(spread_out, ("zh", "zl"), split_axis=0, concat_axis=0, tiled=True)
    pair = jnp.sum(pair.reshape(4, 2, COLS // 16, OWN), axis=0)
    pair = pair.reshape(2, 1, 1, COLS // 16, OWN)
    control_flat = control_wide.reshape(col_rows, 3 * local_cells)
    control_flat, pair = lax.optimization_barrier((control_flat, pair))
    control_all = turned(control_flat)
    left_half = gather_four(pair[..., :LANES], "x", 1)
    right_half = gather_four(pair[..., LANES:], "y", 2)
    left_half = gather_four(left_half, "y", 2).reshape(2, COLS, LANES)
    right_half = gather_four(right_half, "x", 1).reshape(2, COLS, LANES)
    left_other = lax.ppermute(left_half, "core", SWAP)
    right_other = lax.ppermute(right_half, "core", SWAP)
    where = jnp.stack([lax.axis_index(RANK), lax.axis_index("core")]).astype(jnp.int32)
    inverse_low, project_low = factor(where, left_half, right_half, left_other, right_other)
    right_basis = jnp.dot(inverse_low, control_all, preferred_element_type=F32)
    right_basis = right_basis.reshape(control_wide.shape)
    scaled_right = rounded(conducts * right_basis)
    stiff_basis = (-(conduct * stiff_apply(scaled_right.astype(F32)))).astype(BF16)
    left_sum = lax.dot_general(
        project_low, relaid_all, (((1,), (1,)), ((), ())), preferred_element_type=F32
    )
    left_basis = left_sum.astype(BF16).reshape(control.shape)
    return (left_basis, stiff_basis)


def solution(mesh):
    torus = Mesh(mesh.devices.reshape(4, 4, 4, 2, 2), ROWS + RANK)
    in_specs = (
        P(RANK, ROWS, None, None),
        P(RANK, None, ROWS, None),
        P(ROWS, None, None),
        P(ROWS, None, None),
    )
    out_specs = (P(RANK, ROWS, None, None), P(RANK, ROWS, None, None))
    return jax.shard_map(project, mesh=torus, in_specs=in_specs, out_specs=out_specs, check_vma=False)
```

profile of v0, /device:TPU:31, one launch (start us, length us, event | category | flops | bytes accessed | tf_op | source)
XLA Modules:
  0.0 231.2 jit_solution(7522147913857063220)
XLA Ops:
  0.6 4.6 %collective-permute-start = (bf16[256,1,8,128]{3,2,1,0:T(8,128)(2,1)}, bf16[256,1,8,128]{3,2,1,0:T(8,128)(2,1)S(1)}, u32[]{:S(2)}, u32[]{:S(2)}) collective-permute-start(bf16[256,1,8,128]{3,2,1,0:T(8,128)(2,1)} %param.4), channel_id=1, source_target_pairs={{0,4},{4,8},{8,12},{12,16},{16,20},{20,24},{24,28},{28,32},{32,36}... | collective-permute-start | bytes 1572872 | tf_op jit(solution)/shard_map/ppermute | solution.py:27
  7.9 8.5 %collective-permute-start.5 = (f32[2,1,8,128]{3,2,1,0:T(8,128)S(1)}, f32[2,1,8,128]{3,2,1,0:T(8,128)S(1)}, u32[]{:S(2)}, u32[]{:S(2)}) collective-permute-start(f32[2,1,8,128]{3,2,1,0:T(8,128)S(1)} %pad_maximum_fusion.1), channel_id=1, source_target_pairs={{0,4},{4,8},{8,12},{12,16},{16,20},{20,24},{24,28},{28,32},{32,36}... | collective-permute-start | bytes 24584 | tf_op jit(solution)/shard_map/ppermute | solution.py:27
  18.3 2.1 copy.23
  20.4 6.1 %all-to-all-start = ((bf16[16,4,2,8,256]{4,1,2,3,0:T(4,128)(2,1)}), bf16[16,4,2,8,256]{4,1,2,3,0:T(4,128)(2,1)S(1)}, u32[]{:S(2)}, u32[]{:S(2)}) async-start(bf16[16,4,2,8,256]{4,1,2,3,0:T(4,128)(2,1)} %copy.23), calls=%async_computation | async-start | bytes 1048576 | tf_op jit(solution)/shard_map/all_to_all | solution.py:263
  27.5 20.0 %collective-permute-done.1 = bf16[256,1,8,128]{3,2,1,0:T(8,128)(2,1)} collective-permute-done((bf16[256,1,8,128]{3,2,1,0:T(8,128)(2,1)}, bf16[256,1,8,128]{3,2,1,0:T(8,128)(2,1)}, u32[]{:S(2)}, u32[]{:S(2)}) %collective-permute-start.1) | collective-permute-done | bytes 524320 | tf_op jit(solution)/shard_map/ppermute | solution.py:28
  51.9 6.3 %collective-permute-start.2 = (bf16[16,2,8,256]{3,2,1,0:T(8,128)(2,1)S(1)}, bf16[16,2,8,256]{3,2,1,0:T(8,128)(2,1)S(1)}, u32[]{:S(2)}, u32[]{:S(2)}) collective-permute-start(bf16[16,2,8,256]{3,2,1,0:T(8,128)(2,1)S(1)} %bitcast.96), channel_id=1, source_target_pairs={{0,64},{64,128},{128,192},{192,0},{1,65},{65,129},{129,193},{193,1... | collective-permute-start | bytes 393224 | tf_op jit(solution)/shard_map/ppermute | solution.py:272
  59.3 3.5 %collective-permute-start.4 = (bf16[16,2,8,256]{3,2,1,0:T(8,128)(2,1)S(1)}, bf16[16,2,8,256]{3,2,1,0:T(8,128)(2,1)S(1)}, u32[]{:S(2)}, u32[]{:S(2)}) collective-permute-start(bf16[16,2,8,256]{3,2,1,0:T(8,128)(2,1)S(1)} %bitcast.94), channel_id=1, source_target_pairs={{0,192},{64,0},{128,64},{192,128},{1,193},{65,1},{129,65},{193,129... | collective-permute-start | bytes 393224 | tf_op jit(solution)/shard_map/ppermute | solution.py:272
  63.4 3.2 %collective-permute-start.7 = (bf16[256,1024]{1,0:T(8,128)(2,1)S(1)}, bf16[256,1024]{1,0:T(8,128)(2,1)}, u32[]{:S(2)}, u32[]{:S(2)}) collective-permute-start(bf16[256,1024]{1,0:T(8,128)(2,1)S(1)} %bitcast.91), channel_id=1, source_target_pairs={{0,1},{1,0},{2,3},{3,2},{4,5},{5,4},{6,7},{7,6},{8,9},{9,8},{10,11... | collective-permute-start | bytes 1572872 | tf_op jit(solution)/shard_map/ppermute | solution.py:256
  66.6 3.6 %collective-permute-start.9 = (bf16[256,1024]{1,0:T(8,128)(2,1)S(1)}, bf16[256,1024]{1,0:T(8,128)(2,1)}, u32[]{:S(2)}, u32[]{:S(2)}) collective-permute-start(bf16[256,1024]{1,0:T(8,128)(2,1)S(1)} %collective-permute-done.8), channel_id=1, source_target_pairs={{0,1},{1,0},{2,3},{3,2},{4,5},{5,4},{6,7},{7,6},{8,9},{9,8},{10,11... | collective-permute-start | bytes 1572872 | tf_op jit(solution)/shard_map/ppermute | solution.py:257
  70.3 8.3 %collective-permute-done.3 = bf16[16,2,8,256]{3,2,1,0:T(8,128)(2,1)S(1)} collective-permute-done((bf16[16,2,8,256]{3,2,1,0:T(8,128)(2,1)S(1)}, bf16[16,2,8,256]{3,2,1,0:T(8,128)(2,1)S(1)}, u32[]{:S(2)}, u32[]{:S(2)}) %collective-permute-start.3) | collective-permute-done | bytes 131104 | tf_op jit(solution)/shard_map/ppermute | solution.py:272
  79.8 3.1 %fusion.8 = f32[1024,256]{1,0:T(8,128)} fusion(bf16[1024,256]{1,0:T(8,128)(2,1)} %reshape.48, bf16[256,1024]{1,0:T(8,128)(2,1)} %collective-permute-done.9, bf16[256,1024]{1,0:T(8,128)(2,1)S(1)} %collective-permute-done.8, bf16[256,1024]{1,0:T(8,128)(2,1)} %collective-permute-done.7, bf16[256,1024]{1,0:T(8,128)(2,1)S(1)} %bitcast.92), kind=kOutput, calls=%fused_computation.24 | convolution fusion | flops 545259520 | bytes 3670016 | tf_op jit(solution)/shard_map/dot_general | solution.py:297
  82.9 6.1 %all-to-all-start.1 = ((f32[16,64,256]{2,1,0:T(8,128)}), f32[16,64,256]{2,1,0:T(8,128)S(1)}, u32[]{:S(2)}, u32[]{:S(2)}) async-start(f32[16,64,256]{2,1,0:T(8,128)} %bitcast.87), calls=%async_computation.1 | async-start | bytes 2097152 | tf_op jit(solution)/shard_map/all_to_all | solution.py:300
  89.0 11.5 %collective-permute-done.10 = bf16[1024,256]{1,0:T(8,128)(2,1)} collective-permute-done((bf16[1024,256]{1,0:T(8,128)(2,1)}, bf16[1024,256]{1,0:T(8,128)(2,1)}, u32[]{:S(2)}, u32[]{:S(2)}) %collective-permute-start.10) | collective-permute-done | bytes 524320 | tf_op jit(solution)/shard_map/ppermute | solution.py:299
  103.0 3.6 %all-to-all-start.2 = ((f32[8,64,256]{2,1,0:T(8,128)}), f32[8,64,256]{2,1,0:T(8,128)S(1)}, u32[]{:S(2)}, u32[]{:S(2)}) async-start(f32[8,64,256]{2,1,0:T(8,128)} %broadcast_in_dim.35), calls=%async_computation.2 | async-start | bytes 1048576 | tf_op jit(solution)/shard_map/all_to_all | solution.py:305
  108.2 14.5 %all-to-all-done.2 = f32[8,64,256]{2,1,0:T(8,128)S(1)} async-done(((f32[8,64,256]{2,1,0:T(8,128)}), f32[8,64,256]{2,1,0:T(8,128)S(1)}, u32[]{:S(2)}, u32[]{:S(2)}) %all-to-all-start.2) | async-done | bytes 524320 | tf_op jit(solution)/shard_map/all_to_all | solution.py:305
  122.8 2.8 %collective-permute-start.17 = (f32[2,1,1,64,128]{4,3,0,2,1:T(8,128)S(1)}, f32[2,1,1,64,128]{4,3,0,2,1:T(8,128)S(1)}, u32[]{:S(2)}, u32[]{:S(2)}) collective-permute-start(f32[2,1,1,64,128]{4,3,0,2,1:T(8,128)S(1)} %get-tuple-element.36), channel_id=1, source_target_pairs={{0,4},{4,8},{8,12},{12,0},{1,5},{5,9},{9,13},{13,1},{2,6},{6,10},{... | collective-permute-start | bytes 196616 | tf_op jit(solution)/shard_map/ppermute | solution.py:242
  127.4 3.2 %collective-permute-done.19 = f32[2,1,1,64,128]{4,3,0,2,1:T(8,128)S(1)} collective-permute-done((f32[2,1,1,64,128]{4,3,0,2,1:T(8,128)S(1)}, f32[2,1,1,64,128]{4,3,0,2,1:T(8,128)S(1)}, u32[]{:S(2)}, u32[]{:S(2)}) %collective-permute-start.19) | collective-permute-done | bytes 65568 | tf_op jit(solution)/shard_map/ppermute | solution.py:242
  131.5 4.0 %collective-permute-start.15 = (f32[2,4,1,64,128]{4,3,2,1,0:T(8,128)S(1)}, f32[2,4,1,64,128]{4,3,2,1,0:T(8,128)S(1)}, u32[]{:S(2)}, u32[]{:S(2)}) collective-permute-start(f32[2,4,1,64,128]{4,3,2,1,0:T(8,128)S(1)} %bitcast_dynamic-update-slice_fusion.4), channel_id=1, source_target_pairs={{0,8},{4,12},{8,0},{12,4},{1,9},{5,13},{9,1},{13,5},{2,10},{6,14},... | collective-permute-start | bytes 786440 | tf_op jit(solution)/shard_map/ppermute | solution.py:242
  137.8 6.2 %collective-permute-done.21 = f32[2,1,4,64,128]{4,3,2,1,0:T(8,128)S(1)} collective-permute-done((f32[2,1,4,64,128]{4,3,2,1,0:T(8,128)S(1)}, f32[2,1,4,64,128]{4,3,2,1,0:T(8,128)S(1)}, u32[]{:S(2)}, u32[]{:S(2)}) %collective-permute-start.21) | collective-permute-done | bytes 262176 | tf_op jit(solution)/shard_map/ppermute | solution.py:242
  145.1 6.8 %collective-permute-start.24 = (f32[2,1024,128]{2,1,0:T(8,128)S(1)}, f32[2,1024,128]{2,1,0:T(8,128)S(1)}, u32[]{:S(2)}, u32[]{:S(2)}) collective-permute-start(f32[2,1024,128]{2,1,0:T(8,128)S(1)} %bitcast.78), channel_id=1, source_target_pairs={{0,1},{1,0},{2,3},{3,2},{4,5},{5,4},{6,7},{7,6},{8,9},{9,8},{10,11... | collective-permute-start | bytes 3145736 | tf_op jit(solution)/shard_map/ppermute | solution.py:316
  158.4 51.8 %shard_map.59 = (bf16[256,1024]{1,0:T(8,128)(2,1)S(1)}, bf16[256,1024]{1,0:T(8,128)(2,1)S(1)}) custom-call(s32[2]{0:T(128)S(1)} %pad_add_fusion.where, f32[2,1024,128]{2,1,0:T(8,128)S(1)} %bitcast.77, f32[2,1024,128]{2,1,0:T(8,128)S(1)} %bitcast.79, f32[2,1024,128]{2,1,0:T(8,128)S(1)} %copy-done.1, f32[2,1024,128]{2,1,0:T(8,128)S(1)} %collective-permute-done.24.right_other), custom_call_target="tpu_custom_call" | custom-call | tf_op jit(solution)/shard_map/pallas_call | solution.py:220
  210.2 2.3 fusion.32
  213.3 9.4 %collective-permute-done.28 = bf16[256,3072]{1,0:T(8,128)(2,1)} collective-permute-done((bf16[256,3072]{1,0:T(8,128)(2,1)}, bf16[256,3072]{1,0:T(8,128)(2,1)}, u32[]{:S(2)}, u32[]{:S(2)}) %collective-permute-start.28) | collective-permute-done | bytes 1572896 | tf_op jit(solution)/shard_map/ppermute | solution.py:248
  222.7 3.8 %fusion.24 = f32[32,8,24,128]{3,1,2,0:T(8,128)S(1)} fusion(bf16[256,1024]{1,0:T(8,128)(2,1)S(1)} %get-tuple-element.16, bf16[256,3072]{1,0:T(8,128)(2,1)} %collective-permute-done.29, bf16[256,3072]{1,0:T(8,128)(2,1)} %collective-permute-done.28, bf16[256,3072]{1,0:T(8,128)(2,1)} %collective-permute-done.27, bf16[256,3072]{1,0:T(8,128)(2,1)} %bitcast.70), kind=kOutput, calls=%fused_computation.40 | convolution fusion | flops 1635778560 | bytes 9961472 | tf_op jit(solution)/shard_map/dot_general | solution.py:319
  (111 shorter events, 34.9 us)
Async XLA Ops:
  0.6 26.6 %collective-permute-start = (bf16[256,1,8,128]{3,2,1,0:T(8,128)(2,1)}, bf16[256,1,8,128]{3,2,1,0:T(8,128)(2,1)S(1)}, u32[]{:S(2)}, u32[]{:S(2)}) collective-permute-start(bf16[256,1,8,128]{3,2,1,0:T(8,128)(2,1)} %param.4), channel_id=1, source_target_pairs={{0,4},{4,8},{8,12},{12,16},{16,20},{20,24},{24,28},{28,32},{32,36}... | collective-permute-start | bytes 1572872 | tf_op jit(solution)/shard_map/ppermute | solution.py:27
  6.0 20.5 %collective-permute-start.6 = (f32[2,1,8,128]{3,2,1,0:T(8,128)S(1)}, f32[2,1,8,128]{3,2,1,0:T(8,128)S(1)}, u32[]{:S(2)}, u32[]{:S(2)}) collective-permute-start(f32[2,1,8,128]{3,2,1,0:T(8,128)S(1)} %pad_maximum_fusion.1), channel_id=1, source_target_pairs={{4,0},{8,4},{12,8},{16,12},{20,16},{24,20},{28,24},{32,28},{36,32}... | collective-permute-start | bytes 24584 | tf_op jit(solution)/shard_map/ppermute | solution.py:28
  7.9 18.6 %collective-permute-start.5 = (f32[2,1,8,128]{3,2,1,0:T(8,128)S(1)}, f32[2,1,8,128]{3,2,1,0:T(8,128)S(1)}, u32[]{:S(2)}, u32[]{:S(2)}) collective-permute-start(f32[2,1,8,128]{3,2,1,0:T(8,128)S(1)} %pad_maximum_fusion.1), channel_id=1, source_target_pairs={{0,4},{4,8},{8,12},{12,16},{16,20},{20,24},{24,28},{28,32},{32,36}... | collective-permute-start | bytes 24584 | tf_op jit(solution)/shard_map/ppermute | solution.py:27
  16.4 31.1 %collective-permute-start.1 = (bf16[256,1,8,128]{3,2,1,0:T(8,128)(2,1)}, bf16[256,1,8,128]{3,2,1,0:T(8,128)(2,1)}, u32[]{:S(2)}, u32[]{:S(2)}) collective-permute-start(bf16[256,1,8,128]{3,2,1,0:T(8,128)(2,1)} %param.4), channel_id=1, source_target_pairs={{4,0},{8,4},{12,8},{16,12},{20,16},{24,20},{28,24},{32,28},{36,32}... | collective-permute-start | bytes 1572872 | tf_op jit(solution)/shard_map/ppermute | solution.py:28
  20.4 30.1 %all-to-all-start = ((bf16[16,4,2,8,256]{4,1,2,3,0:T(4,128)(2,1)}), bf16[16,4,2,8,256]{4,1,2,3,0:T(4,128)(2,1)S(1)}, u32[]{:S(2)}, u32[]{:S(2)}) async-start(bf16[16,4,2,8,256]{4,1,2,3,0:T(4,128)(2,1)} %copy.23), calls=%async_computation | async-start | bytes 1048576 | tf_op jit(solution)/shard_map/all_to_all | solution.py:263
  50.3 16.3 %collective-permute-start.8 = (bf16[256,1024]{1,0:T(8,128)(2,1)S(1)}, bf16[256,1024]{1,0:T(8,128)(2,1)S(1)}, u32[]{:S(2)}, u32[]{:S(2)}) collective-permute-start(bf16[256,1024]{1,0:T(8,128)(2,1)S(1)} %bitcast.90), channel_id=1, source_target_pairs={{0,2},{2,0},{1,3},{3,1},{4,6},{6,4},{5,7},{7,5},{8,10},{10,8},{9,1... | collective-permute-start | bytes 1572872 | tf_op jit(solution)/shard_map/ppermute | solution.py:296
  51.9 18.3 %collective-permute-start.2 = (bf16[16,2,8,256]{3,2,1,0:T(8,128)(2,1)S(1)}, bf16[16,2,8,256]{3,2,1,0:T(8,128)(2,1)S(1)}, u32[]{:S(2)}, u32[]{:S(2)}) collective-permute-start(bf16[16,2,8,256]{3,2,1,0:T(8,128)(2,1)S(1)} %bitcast.96), channel_id=1, source_target_pairs={{0,64},{64,128},{128,192},{192,0},{1,65},{65,129},{129,193},{193,1... | collective-permute-start | bytes 393224 | tf_op jit(solution)/shard_map/ppermute | solution.py:272
  58.2 20.4 %collective-permute-start.3 = (bf16[16,2,8,256]{3,2,1,0:T(8,128)(2,1)S(1)}, bf16[16,2,8,256]{3,2,1,0:T(8,128)(2,1)S(1)}, u32[]{:S(2)}, u32[]{:S(2)}) collective-permute-start(bf16[16,2,8,256]{3,2,1,0:T(8,128)(2,1)S(1)} %bitcast.95), channel_id=1, source_target_pairs={{0,128},{64,192},{128,0},{192,64},{1,129},{65,193},{129,1},{193,65... | collective-permute-start | bytes 393224 | tf_op jit(solution)/shard_map/ppermute | solution.py:272
  59.3 19.4 %collective-permute-start.4 = (bf16[16,2,8,256]{3,2,1,0:T(8,128)(2,1)S(1)}, bf16[16,2,8,256]{3,2,1,0:T(8,128)(2,1)S(1)}, u32[]{:S(2)}, u32[]{:S(2)}) collective-permute-start(bf16[16,2,8,256]{3,2,1,0:T(8,128)(2,1)S(1)} %bitcast.94), channel_id=1, source_target_pairs={{0,192},{64,0},{128,64},{192,128},{1,193},{65,1},{129,65},{193,129... | collective-permute-start | bytes 393224 | tf_op jit(solution)/shard_map/ppermute | solution.py:272
  63.4 16.5 %collective-permute-start.7 = (bf16[256,1024]{1,0:T(8,128)(2,1)S(1)}, bf16[256,1024]{1,0:T(8,128)(2,1)}, u32[]{:S(2)}, u32[]{:S(2)}) collective-permute-start(bf16[256,1024]{1,0:T(8,128)(2,1)S(1)} %bitcast.91), channel_id=1, source_target_pairs={{0,1},{1,0},{2,3},{3,2},{4,5},{5,4},{6,7},{7,6},{8,9},{9,8},{10,11... | collective-permute-start | bytes 1572872 | tf_op jit(solution)/shard_map/ppermute | solution.py:256
  66.6 13.2 %collective-permute-start.9 = (bf16[256,1024]{1,0:T(8,128)(2,1)S(1)}, bf16[256,1024]{1,0:T(8,128)(2,1)}, u32[]{:S(2)}, u32[]{:S(2)}) collective-permute-start(bf16[256,1024]{1,0:T(8,128)(2,1)S(1)} %collective-permute-done.8), channel_id=1, source_target_pairs={{0,1},{1,0},{2,3},{3,2},{4,5},{5,4},{6,7},{7,6},{8,9},{9,8},{10,11... | collective-permute-start | bytes 1572872 | tf_op jit(solution)/shard_map/ppermute | solution.py:257
  82.9 19.2 %all-to-all-start.1 = ((f32[16,64,256]{2,1,0:T(8,128)}), f32[16,64,256]{2,1,0:T(8,128)S(1)}, u32[]{:S(2)}, u32[]{:S(2)}) async-start(f32[16,64,256]{2,1,0:T(8,128)} %bitcast.87), calls=%async_computation.1 | async-start | bytes 2097152 | tf_op jit(solution)/shard_map/all_to_all | solution.py:300
  89.0 11.5 %collective-permute-start.10 = (bf16[1024,256]{1,0:T(8,128)(2,1)}, bf16[1024,256]{1,0:T(8,128)(2,1)}, u32[]{:S(2)}, u32[]{:S(2)}) collective-permute-start(bf16[1024,256]{1,0:T(8,128)(2,1)} %reshape.48), channel_id=1, source_target_pairs={{0,2},{2,0},{1,3},{3,1},{4,6},{6,4},{5,7},{7,5},{8,10},{10,8},{9,1... | collective-permute-start | bytes 1572872 | tf_op jit(solution)/shard_map/ppermute | solution.py:299
  103.0 19.6 %all-to-all-start.2 = ((f32[8,64,256]{2,1,0:T(8,128)}), f32[8,64,256]{2,1,0:T(8,128)S(1)}, u32[]{:S(2)}, u32[]{:S(2)}) async-start(f32[8,64,256]{2,1,0:T(8,128)} %broadcast_in_dim.35), calls=%async_computation.2 | async-start | bytes 1048576 | tf_op jit(solution)/shard_map/all_to_all | solution.py:305
  131.3 20.7 %collective-permute-start.16 = (f32[2,4,1,64,128]{4,3,2,1,0:T(8,128)S(1)}, f32[2,4,1,64,128]{4,3,2,1,0:T(8,128)S(1)}, u32[]{:S(2)}, u32[]{:S(2)}) collective-permute-start(f32[2,4,1,64,128]{4,3,2,1,0:T(8,128)S(1)} %bitcast_dynamic-update-slice_fusion.4), channel_id=1, source_target_pairs={{0,12},{4,0},{8,4},{12,8},{1,13},{5,1},{9,5},{13,9},{2,14},{6,2},{... | collective-permute-start | bytes 786440 | tf_op jit(solution)/shard_map/ppermute | solution.py:242
  131.5 20.4 %collective-permute-start.15 = (f32[2,4,1,64,128]{4,3,2,1,0:T(8,128)S(1)}, f32[2,4,1,64,128]{4,3,2,1,0:T(8,128)S(1)}, u32[]{:S(2)}, u32[]{:S(2)}) collective-permute-start(f32[2,4,1,64,128]{4,3,2,1,0:T(8,128)S(1)} %bitcast_dynamic-update-slice_fusion.4), channel_id=1, source_target_pairs={{0,8},{4,12},{8,0},{12,4},{1,9},{5,13},{9,1},{13,5},{2,10},{6,14},... | collective-permute-start | bytes 786440 | tf_op jit(solution)/shard_map/ppermute | solution.py:242
  135.6 9.5 %collective-permute-start.22 = (f32[2,1,4,64,128]{4,3,2,1,0:T(8,128)S(1)}, f32[2,1,4,64,128]{4,3,2,1,0:T(8,128)S(1)}, u32[]{:S(2)}, u32[]{:S(2)}) collective-permute-start(f32[2,1,4,64,128]{4,3,2,1,0:T(8,128)S(1)} %bitcast_dynamic-update-slice_fusion), channel_id=1, source_target_pairs={{0,48},{16,0},{32,16},{48,32},{1,49},{17,1},{33,17},{49,33},{2,50}... | collective-permute-start | bytes 786440 | tf_op jit(solution)/shard_map/ppermute | solution.py:242
  137.6 14.3 %collective-permute-start.14 = (f32[2,4,1,64,128]{4,3,2,1,0:T(8,128)S(1)}, f32[2,4,1,64,128]{4,3,2,1,0:T(8,128)S(1)}, u32[]{:S(2)}, u32[]{:S(2)}) collective-permute-start(f32[2,4,1,64,128]{4,3,2,1,0:T(8,128)S(1)} %bitcast_dynamic-update-slice_fusion.4), channel_id=1, source_target_pairs={{0,4},{4,8},{8,12},{12,0},{1,5},{5,9},{9,13},{13,1},{2,6},{6,10},{... | collective-permute-start | bytes 786440 | tf_op jit(solution)/shard_map/ppermute | solution.py:242
  145.1 9.2 %collective-permute-start.24 = (f32[2,1024,128]{2,1,0:T(8,128)S(1)}, f32[2,1024,128]{2,1,0:T(8,128)S(1)}, u32[]{:S(2)}, u32[]{:S(2)}) collective-permute-start(f32[2,1024,128]{2,1,0:T(8,128)S(1)} %bitcast.78), channel_id=1, source_target_pairs={{0,1},{1,0},{2,3},{3,2},{4,5},{5,4},{6,7},{7,6},{8,9},{9,8},{10,11... | collective-permute-start | bytes 3145736 | tf_op jit(solution)/shard_map/ppermute | solution.py:316
  152.2 61.2 %collective-permute-start.29 = (bf16[256,3072]{1,0:T(8,128)(2,1)}, bf16[256,3072]{1,0:T(8,128)(2,1)}, u32[]{:S(2)}, u32[]{:S(2)}) collective-permute-start(bf16[256,3072]{1,0:T(8,128)(2,1)} %bitcast.70), channel_id=1, source_target_pairs={{0,3},{1,2},{2,1},{3,0},{4,7},{5,6},{6,5},{7,4},{8,11},{9,10},{10,... | collective-permute-start | bytes 4718600 | tf_op jit(solution)/shard_map/ppermute | solution.py:248
  153.5 69.2 %collective-permute-start.28 = (bf16[256,3072]{1,0:T(8,128)(2,1)}, bf16[256,3072]{1,0:T(8,128)(2,1)}, u32[]{:S(2)}, u32[]{:S(2)}) collective-permute-start(bf16[256,3072]{1,0:T(8,128)(2,1)} %bitcast.70), channel_id=1, source_target_pairs={{0,2},{1,3},{2,0},{3,1},{4,6},{5,7},{6,4},{7,5},{8,10},{9,11},{10,... | collective-permute-start | bytes 4718600 | tf_op jit(solution)/shard_map/ppermute | solution.py:248
  154.0 68.7 %collective-permute-start.27 = (bf16[256,3072]{1,0:T(8,128)(2,1)}, bf16[256,3072]{1,0:T(8,128)(2,1)}, u32[]{:S(2)}, u32[]{:S(2)}) collective-permute-start(bf16[256,3072]{1,0:T(8,128)(2,1)} %bitcast.70), channel_id=1, source_target_pairs={{0,1},{1,0},{2,3},{3,2},{4,5},{5,4},{6,7},{7,6},{8,9},{9,8},{10,11... | collective-permute-start | bytes 4718600 | tf_op jit(solution)/shard_map/ppermute | solution.py:248
  154.4 55.8 %collective-permute-start.25 = (bf16[1024,256]{1,0:T(8,128)(2,1)}, bf16[1024,256]{1,0:T(8,128)(2,1)}, u32[]{:S(2)}, u32[]{:S(2)}) collective-permute-start(bf16[1024,256]{1,0:T(8,128)(2,1)} %reshape.48), channel_id=1, source_target_pairs={{0,1},{1,0},{2,3},{3,2},{4,5},{5,4},{6,7},{7,6},{8,9},{9,8},{10,11... | collective-permute-start | bytes 1572872 | tf_op jit(solution)/shard_map/ppermute | solution.py:256
  156.7 53.5 %collective-permute-start.26 = (bf16[1024,256]{1,0:T(8,128)(2,1)}, bf16[1024,256]{1,0:T(8,128)(2,1)}, u32[]{:S(2)}, u32[]{:S(2)}) collective-permute-start(bf16[1024,256]{1,0:T(8,128)(2,1)} %collective-permute-done.10), channel_id=1, source_target_pairs={{0,1},{1,0},{2,3},{3,2},{4,5},{5,4},{6,7},{7,6},{8,9},{9,8},{10,11... | collective-permute-start | bytes 1572872 | tf_op jit(solution)/shard_map/ppermute | solution.py:257
  (14 other events, 78.9 us)
where the time goes:
time: 235 us; the launch traced here: 231 us
  waiting for transfers between devices  78.5 us (33%)
  starting transfers between devices  69.9 us (30%)
  Pallas kernels  51.8 us (22%)
  local copies, waits for them, and re-layouts  13.6 us (6%)
  matrix products  9.16 us (4%)
  other arithmetic  7.05 us (3%)
    pallas_call x1, Pallas kernels, factor(): pl.pallas_call(factor_kernel, out_shape=(jax.ShapeDtypeStruct((OWN, COLS)...  51.8 us
    ppermute x2, waiting for transfers between devices, neighbours(): after = lax.ppermute(x, ROWS, down)  20 us
    all_to_all x1, waiting for transfers between devices, project(): lax.all_to_all(spread_out, ('zh', 'zl'), split_axis=0, concat_axis=0, til...  14.5 us
    ppermute x2, starting transfers between devices, neighbours(): before = lax.ppermute(x, ROWS, up)  13.1 us
    ppermute x12, waiting for transfers between devices, gather_four(): moved = lax.ppermute(x, axis, [(d, (d + step) % 4) for d in range(4)])  12.1 us
    ppermute x1, waiting for transfers between devices, project(): across = lax.ppermute(relaid, 'zl', SWAP)  11.5 us
    ppermute x3, starting transfers between devices, replane(): lax.ppermute(leaving, 'zh', [(d, (d + step) % 4) for d in range(4)])  10.9 us
    ppermute x12, starting transfers between devices, gather_four(): moved = lax.ppermute(x, axis, [(d, (d + step) % 4) for d in range(4)])  9.76 us
  transfers between devices with their start and end apart: 33, of which 13 were waited for; matrix products, arithmetic and copies ran while one was open for 6% of the time, Pallas kernels for 22%

commit v1 on v0

--- a/solution.py
+++ b/solution.py
@@ -126,7 +126,7 @@
     return jnp.concatenate(out, axis=0)
 
 
-def factor_kernel(where, left, right, left_other, right_other, inv_out, proj_out, high, low, m, r_high, r_low):
+def factor_kernel(where, left, right, left_other, right_other, inv_out, proj_out, high, low, m, r_left, r_right):
     core = where[1]
     strip = OWN // 4
 
@@ -178,14 +178,17 @@
         r = product(halves(x), halves(m[block, :]))
         m[block, :] = r
         upper, lower = halves(r)
-        r_high[...] = upper
-        r_low[...] = lower
+        for at, (one, two) in enumerate(((upper, upper), (upper, lower), (lower, upper))):
+            r_left[at * SIDE : (at + 1) * SIDE, :] = one
+            r_right[at * SIDE : (at + 1) * SIDE, :] = two
 
         def update(i, inner):
             rows = pl.ds(pl.multiple_of(i * SIDE, SIDE), SIDE)
             m[rows, block] = jnp.zeros((SIDE, SIDE), F32)
-            mine = (r_high[:, rows], r_low[:, rows])
-            m[rows, :] = m[rows, :] - product(mine, (r_high[...], r_low[...]), 0, 0)
+            taken = lax.dot_general(
+                r_left[:, rows], r_right[...], (((0,), (0,)), ((), ())), preferred_element_type=F32
+            )
+            m[rows, :] = m[rows, :] - taken
             return inner
 
         lax.fori_loop(k + 1, TILES, update, 0)
@@ -226,8 +229,8 @@
             pltpu.VMEM((COLS, COLS), BF16),
             pltpu.VMEM((COLS, COLS), BF16),
             pltpu.VMEM((COLS, COLS), F32),
-            pltpu.VMEM((SIDE, COLS), BF16),
-            pltpu.VMEM((SIDE, COLS), BF16),
+            pltpu.VMEM((3 * SIDE, COLS), BF16),
+            pltpu.VMEM((3 * SIDE, COLS), BF16),
         ],
         compiler_params=pltpu.CompilerParams(vmem_limit_bytes=20 * 2**20),
     )(where, left, right, left_other, right_other)

time: 235 us -> 235 us (level)
  no operation moved by 1% of the time
where the time goes in v1:
time: 235 us; the launch traced here: 231 us
  waiting for transfers between devices  79.5 us (34%)
  starting transfers between devices  69.9 us (30%)
  Pallas kernels  50.8 us (22%)
  local copies, waits for them, and re-layouts  13.6 us (6%)
  matrix products  9.16 us (4%)
  other arithmetic  7.05 us (3%)
    pallas_call x1, Pallas kernels, factor(): pl.pallas_call(factor_kernel, out_shape=(jax.ShapeDtypeStruct((OWN, COLS)...  50.8 us
    ppermute x2, waiting for transfers between devices, neighbours(): after = lax.ppermute(x, ROWS, down)  20 us
    all_to_all x1, waiting for transfers between devices, project(): lax.all_to_all(spread_out, ('zh', 'zl'), split_axis=0, concat_axis=0, til...  14.5 us
    ppermute x2, starting transfers between devices, neighbours(): before = lax.ppermute(x, ROWS, up)  13.1 us
    ppermute x12, waiting for transfers between devices, gather_four(): moved = lax.ppermute(x, axis, [(d, (d + step) % 4) for d in range(4)])  12.1 us
    ppermute x1, waiting for transfers between devices, project(): across = lax.ppermute(relaid, 'zl', SWAP)  11.5 us
    ppermute x3, starting transfers between devices, replane(): lax.ppermute(leaving, 'zh', [(d, (d + step) % 4) for d in range(4)])  10.9 us
    ppermute x3, waiting for transfers between devices, turned(): lax.ppermute(x, RANK, [(d, d ^ step) for d in range(4)])  10.3 us
  transfers between devices with their start and end apart: 33, of which 13 were waited for; matrix products, arithmetic and copies ran while one was open for 6% of the time, Pallas kernels for 22%

profile of v1, /device:TPU:31, one launch (start us, length us, event | category | flops | bytes accessed | tf_op | source)
XLA Modules:
  0.0 231.2 jit_solution(15954975029742698868)
XLA Ops:
  0.6 4.6 %collective-permute-start = (bf16[256,1,8,128]{3,2,1,0:T(8,128)(2,1)}, bf16[256,1,8,128]{3,2,1,0:T(8,128)(2,1)S(1)}, u32[]{:S(2)}, u32[]{:S(2)}) collective-permute-start(bf16[256,1,8,128]{3,2,1,0:T(8,128)(2,1)} %param.4), channel_id=1, source_target_pairs={{0,4},{4,8},{8,12},{12,16},{16,20},{20,24},{24,28},{28,32},{32,36}... | collective-permute-start | bytes 1572872 | tf_op jit(solution)/shard_map/ppermute | solution.py:27
  7.9 8.5 %collective-permute-start.5 = (f32[2,1,8,128]{3,2,1,0:T(8,128)S(1)}, f32[2,1,8,128]{3,2,1,0:T(8,128)S(1)}, u32[]{:S(2)}, u32[]{:S(2)}) collective-permute-start(f32[2,1,8,128]{3,2,1,0:T(8,128)S(1)} %pad_maximum_fusion.1), channel_id=1, source_target_pairs={{0,4},{4,8},{8,12},{12,16},{16,20},{20,24},{24,28},{28,32},{32,36}... | collective-permute-start | bytes 24584 | tf_op jit(solution)/shard_map/ppermute | solution.py:27
  18.3 2.1 copy.23
  20.4 6.1 %all-to-all-start = ((bf16[16,4,2,8,256]{4,1,2,3,0:T(4,128)(2,1)}), bf16[16,4,2,8,256]{4,1,2,3,0:T(4,128)(2,1)S(1)}, u32[]{:S(2)}, u32[]{:S(2)}) async-start(bf16[16,4,2,8,256]{4,1,2,3,0:T(4,128)(2,1)} %copy.23), calls=%async_computation | async-start | bytes 1048576 | tf_op jit(solution)/shard_map/all_to_all | solution.py:266
  27.5 20.0 %collective-permute-done.1 = bf16[256,1,8,128]{3,2,1,0:T(8,128)(2,1)} collective-permute-done((bf16[256,1,8,128]{3,2,1,0:T(8,128)(2,1)}, bf16[256,1,8,128]{3,2,1,0:T(8,128)(2,1)}, u32[]{:S(2)}, u32[]{:S(2)}) %collective-permute-start.1) | collective-permute-done | bytes 524320 | tf_op jit(solution)/shard_map/ppermute | solution.py:28
  51.9 6.3 %collective-permute-start.2 = (bf16[16,2,8,256]{3,2,1,0:T(8,128)(2,1)S(1)}, bf16[16,2,8,256]{3,2,1,0:T(8,128)(2,1)S(1)}, u32[]{:S(2)}, u32[]{:S(2)}) collective-permute-start(bf16[16,2,8,256]{3,2,1,0:T(8,128)(2,1)S(1)} %bitcast.96), channel_id=1, source_target_pairs={{0,64},{64,128},{128,192},{192,0},{1,65},{65,129},{129,193},{193,1... | collective-permute-start | bytes 393224 | tf_op jit(solution)/shard_map/ppermute | solution.py:275
  59.3 3.5 %collective-permute-start.4 = (bf16[16,2,8,256]{3,2,1,0:T(8,128)(2,1)S(1)}, bf16[16,2,8,256]{3,2,1,0:T(8,128)(2,1)S(1)}, u32[]{:S(2)}, u32[]{:S(2)}) collective-permute-start(bf16[16,2,8,256]{3,2,1,0:T(8,128)(2,1)S(1)} %bitcast.94), channel_id=1, source_target_pairs={{0,192},{64,0},{128,64},{192,128},{1,193},{65,1},{129,65},{193,129... | collective-permute-start | bytes 393224 | tf_op jit(solution)/shard_map/ppermute | solution.py:275
  63.4 3.2 %collective-permute-start.7 = (bf16[256,1024]{1,0:T(8,128)(2,1)S(1)}, bf16[256,1024]{1,0:T(8,128)(2,1)}, u32[]{:S(2)}, u32[]{:S(2)}) collective-permute-start(bf16[256,1024]{1,0:T(8,128)(2,1)S(1)} %bitcast.91), channel_id=1, source_target_pairs={{0,1},{1,0},{2,3},{3,2},{4,5},{5,4},{6,7},{7,6},{8,9},{9,8},{10,11... | collective-permute-start | bytes 1572872 | tf_op jit(solution)/shard_map/ppermute | solution.py:259
  66.6 3.6 %collective-permute-start.9 = (bf16[256,1024]{1,0:T(8,128)(2,1)S(1)}, bf16[256,1024]{1,0:T(8,128)(2,1)}, u32[]{:S(2)}, u32[]{:S(2)}) collective-permute-start(bf16[256,1024]{1,0:T(8,128)(2,1)S(1)} %collective-permute-done.8), channel_id=1, source_target_pairs={{0,1},{1,0},{2,3},{3,2},{4,5},{5,4},{6,7},{7,6},{8,9},{9,8},{10,11... | collective-permute-start | bytes 1572872 | tf_op jit(solution)/shard_map/ppermute | solution.py:260
  70.3 8.3 %collective-permute-done.3 = bf16[16,2,8,256]{3,2,1,0:T(8,128)(2,1)S(1)} collective-permute-done((bf16[16,2,8,256]{3,2,1,0:T(8,128)(2,1)S(1)}, bf16[16,2,8,256]{3,2,1,0:T(8,128)(2,1)S(1)}, u32[]{:S(2)}, u32[]{:S(2)}) %collective-permute-start.3) | collective-permute-done | bytes 131104 | tf_op jit(solution)/shard_map/ppermute | solution.py:275
  79.8 3.1 %fusion.8 = f32[1024,256]{1,0:T(8,128)} fusion(bf16[1024,256]{1,0:T(8,128)(2,1)} %reshape.48, bf16[256,1024]{1,0:T(8,128)(2,1)} %collective-permute-done.9, bf16[256,1024]{1,0:T(8,128)(2,1)S(1)} %collective-permute-done.8, bf16[256,1024]{1,0:T(8,128)(2,1)} %collective-permute-done.7, bf16[256,1024]{1,0:T(8,128)(2,1)S(1)} %bitcast.92), kind=kOutput, calls=%fused_computation.24 | convolution fusion | flops 545259520 | bytes 3670016 | tf_op jit(solution)/shard_map/dot_general | solution.py:300
  82.9 6.1 %all-to-all-start.1 = ((f32[16,64,256]{2,1,0:T(8,128)}), f32[16,64,256]{2,1,0:T(8,128)S(1)}, u32[]{:S(2)}, u32[]{:S(2)}) async-start(f32[16,64,256]{2,1,0:T(8,128)} %bitcast.87), calls=%async_computation.1 | async-start | bytes 2097152 | tf_op jit(solution)/shard_map/all_to_all | solution.py:303
  89.0 11.5 %collective-permute-done.10 = bf16[1024,256]{1,0:T(8,128)(2,1)} collective-permute-done((bf16[1024,256]{1,0:T(8,128)(2,1)}, bf16[1024,256]{1,0:T(8,128)(2,1)}, u32[]{:S(2)}, u32[]{:S(2)}) %collective-permute-start.10) | collective-permute-done | bytes 524320 | tf_op jit(solution)/shard_map/ppermute | solution.py:302
  103.0 3.6 %all-to-all-start.2 = ((f32[8,64,256]{2,1,0:T(8,128)}), f32[8,64,256]{2,1,0:T(8,128)S(1)}, u32[]{:S(2)}, u32[]{:S(2)}) async-start(f32[8,64,256]{2,1,0:T(8,128)} %broadcast_in_dim.35), calls=%async_computation.2 | async-start | bytes 1048576 | tf_op jit(solution)/shard_map/all_to_all | solution.py:308
  108.2 14.5 %all-to-all-done.2 = f32[8,64,256]{2,1,0:T(8,128)S(1)} async-done(((f32[8,64,256]{2,1,0:T(8,128)}), f32[8,64,256]{2,1,0:T(8,128)S(1)}, u32[]{:S(2)}, u32[]{:S(2)}) %all-to-all-start.2) | async-done | bytes 524320 | tf_op jit(solution)/shard_map/all_to_all | solution.py:308
  122.8 2.8 %collective-permute-start.17 = (f32[2,1,1,64,128]{4,3,0,2,1:T(8,128)S(1)}, f32[2,1,1,64,128]{4,3,0,2,1:T(8,128)S(1)}, u32[]{:S(2)}, u32[]{:S(2)}) collective-permute-start(f32[2,1,1,64,128]{4,3,0,2,1:T(8,128)S(1)} %get-tuple-element.36), channel_id=1, source_target_pairs={{0,4},{4,8},{8,12},{12,0},{1,5},{5,9},{9,13},{13,1},{2,6},{6,10},{... | collective-permute-start | bytes 196616 | tf_op jit(solution)/shard_map/ppermute | solution.py:245
  127.4 3.2 %collective-permute-done.19 = f32[2,1,1,64,128]{4,3,0,2,1:T(8,128)S(1)} collective-permute-done((f32[2,1,1,64,128]{4,3,0,2,1:T(8,128)S(1)}, f32[2,1,1,64,128]{4,3,0,2,1:T(8,128)S(1)}, u32[]{:S(2)}, u32[]{:S(2)}) %collective-permute-start.19) | collective-permute-done | bytes 65568 | tf_op jit(solution)/shard_map/ppermute | solution.py:245
  131.5 4.0 %collective-permute-start.15 = (f32[2,4,1,64,128]{4,3,2,1,0:T(8,128)S(1)}, f32[2,4,1,64,128]{4,3,2,1,0:T(8,128)S(1)}, u32[]{:S(2)}, u32[]{:S(2)}) collective-permute-start(f32[2,4,1,64,128]{4,3,2,1,0:T(8,128)S(1)} %bitcast_dynamic-update-slice_fusion.4), channel_id=1, source_target_pairs={{0,8},{4,12},{8,0},{12,4},{1,9},{5,13},{9,1},{13,5},{2,10},{6,14},... | collective-permute-start | bytes 786440 | tf_op jit(solution)/shard_map/ppermute | solution.py:245
  137.8 6.2 %collective-permute-done.21 = f32[2,1,4,64,128]{4,3,2,1,0:T(8,128)S(1)} collective-permute-done((f32[2,1,4,64,128]{4,3,2,1,0:T(8,128)S(1)}, f32[2,1,4,64,128]{4,3,2,1,0:T(8,128)S(1)}, u32[]{:S(2)}, u32[]{:S(2)}) %collective-permute-start.21) | collective-permute-done | bytes 262176 | tf_op jit(solution)/shard_map/ppermute | solution.py:245
  145.1 6.8 %collective-permute-start.24 = (f32[2,1024,128]{2,1,0:T(8,128)S(1)}, f32[2,1024,128]{2,1,0:T(8,128)S(1)}, u32[]{:S(2)}, u32[]{:S(2)}) collective-permute-start(f32[2,1024,128]{2,1,0:T(8,128)S(1)} %bitcast.78), channel_id=1, source_target_pairs={{0,1},{1,0},{2,3},{3,2},{4,5},{5,4},{6,7},{7,6},{8,9},{9,8},{10,11... | collective-permute-start | bytes 3145736 | tf_op jit(solution)/shard_map/ppermute | solution.py:319
  158.4 50.8 %shard_map.59 = (bf16[256,1024]{1,0:T(8,128)(2,1)S(1)}, bf16[256,1024]{1,0:T(8,128)(2,1)S(1)}) custom-call(s32[2]{0:T(128)S(1)} %pad_add_fusion.where, f32[2,1024,128]{2,1,0:T(8,128)S(1)} %bitcast.77, f32[2,1024,128]{2,1,0:T(8,128)S(1)} %bitcast.79, f32[2,1024,128]{2,1,0:T(8,128)S(1)} %copy-done.1, f32[2,1024,128]{2,1,0:T(8,128)S(1)} %collective-permute-done.24.right_other), custom_call_target="tpu_custom_call" | custom-call | tf_op jit(solution)/shard_map/pallas_call | solution.py:223
  209.2 2.3 fusion.32
  212.3 10.3 %collective-permute-done.28 = bf16[256,3072]{1,0:T(8,128)(2,1)} collective-permute-done((bf16[256,3072]{1,0:T(8,128)(2,1)}, bf16[256,3072]{1,0:T(8,128)(2,1)}, u32[]{:S(2)}, u32[]{:S(2)}) %collective-permute-start.28) | collective-permute-done | bytes 1572896 | tf_op jit(solution)/shard_map/ppermute | solution.py:251
  222.7 3.8 %fusion.24 = f32[32,8,24,128]{3,1,2,0:T(8,128)S(1)} fusion(bf16[256,1024]{1,0:T(8,128)(2,1)S(1)} %get-tuple-element.16, bf16[256,3072]{1,0:T(8,128)(2,1)} %collective-permute-done.29, bf16[256,3072]{1,0:T(8,128)(2,1)} %collective-permute-done.28, bf16[256,3072]{1,0:T(8,128)(2,1)} %collective-permute-done.27, bf16[256,3072]{1,0:T(8,128)(2,1)} %bitcast.70), kind=kOutput, calls=%fused_computation.40 | convolution fusion | flops 1635778560 | bytes 9961472 | tf_op jit(solution)/shard_map/dot_general | solution.py:322
  (111 shorter events, 34.9 us)
Async XLA Ops:
  0.6 26.6 %collective-permute-start = (bf16[256,1,8,128]{3,2,1,0:T(8,128)(2,1)}, bf16[256,1,8,128]{3,2,1,0:T(8,128)(2,1)S(1)}, u32[]{:S(2)}, u32[]{:S(2)}) collective-permute-start(bf16[256,1,8,128]{3,2,1,0:T(8,128)(2,1)} %param.4), channel_id=1, source_target_pairs={{0,4},{4,8},{8,12},{12,16},{16,20},{20,24},{24,28},{28,32},{32,36}... | collective-permute-start | bytes 1572872 | tf_op jit(solution)/shard_map/ppermute | solution.py:27
  6.0 20.5 %collective-permute-start.6 = (f32[2,1,8,128]{3,2,1,0:T(8,128)S(1)}, f32[2,1,8,128]{3,2,1,0:T(8,128)S(1)}, u32[]{:S(2)}, u32[]{:S(2)}) collective-permute-start(f32[2,1,8,128]{3,2,1,0:T(8,128)S(1)} %pad_maximum_fusion.1), channel_id=1, source_target_pairs={{4,0},{8,4},{12,8},{16,12},{20,16},{24,20},{28,24},{32,28},{36,32}... | collective-permute-start | bytes 24584 | tf_op jit(solution)/shard_map/ppermute | solution.py:28
  7.9 18.6 %collective-permute-start.5 = (f32[2,1,8,128]{3,2,1,0:T(8,128)S(1)}, f32[2,1,8,128]{3,2,1,0:T(8,128)S(1)}, u32[]{:S(2)}, u32[]{:S(2)}) collective-permute-start(f32[2,1,8,128]{3,2,1,0:T(8,128)S(1)} %pad_maximum_fusion.1), channel_id=1, source_target_pairs={{0,4},{4,8},{8,12},{12,16},{16,20},{20,24},{24,28},{28,32},{32,36}... | collective-permute-start | bytes 24584 | tf_op jit(solution)/shard_map/ppermute | solution.py:27
  16.4 31.1 %collective-permute-start.1 = (bf16[256,1,8,128]{3,2,1,0:T(8,128)(2,1)}, bf16[256,1,8,128]{3,2,1,0:T(8,128)(2,1)}, u32[]{:S(2)}, u32[]{:S(2)}) collective-permute-start(bf16[256,1,8,128]{3,2,1,0:T(8,128)(2,1)} %param.4), channel_id=1, source_target_pairs={{4,0},{8,4},{12,8},{16,12},{20,16},{24,20},{28,24},{32,28},{36,32}... | collective-permute-start | bytes 1572872 | tf_op jit(solution)/shard_map/ppermute | solution.py:28
  20.4 30.1 %all-to-all-start = ((bf16[16,4,2,8,256]{4,1,2,3,0:T(4,128)(2,1)}), bf16[16,4,2,8,256]{4,1,2,3,0:T(4,128)(2,1)S(1)}, u32[]{:S(2)}, u32[]{:S(2)}) async-start(bf16[16,4,2,8,256]{4,1,2,3,0:T(4,128)(2,1)} %copy.23), calls=%async_computation | async-start | bytes 1048576 | tf_op jit(solution)/shard_map/all_to_all | solution.py:266
  50.3 16.3 %collective-permute-start.8 = (bf16[256,1024]{1,0:T(8,128)(2,1)S(1)}, bf16[256,1024]{1,0:T(8,128)(2,1)S(1)}, u32[]{:S(2)}, u32[]{:S(2)}) collective-permute-start(bf16[256,1024]{1,0:T(8,128)(2,1)S(1)} %bitcast.90), channel_id=1, source_target_pairs={{0,2},{2,0},{1,3},{3,1},{4,6},{6,4},{5,7},{7,5},{8,10},{10,8},{9,1... | collective-permute-start | bytes 1572872 | tf_op jit(solution)/shard_map/ppermute | solution.py:299
  51.9 18.3 %collective-permute-start.2 = (bf16[16,2,8,256]{3,2,1,0:T(8,128)(2,1)S(1)}, bf16[16,2,8,256]{3,2,1,0:T(8,128)(2,1)S(1)}, u32[]{:S(2)}, u32[]{:S(2)}) collective-permute-start(bf16[16,2,8,256]{3,2,1,0:T(8,128)(2,1)S(1)} %bitcast.96), channel_id=1, source_target_pairs={{0,64},{64,128},{128,192},{192,0},{1,65},{65,129},{129,193},{193,1... | collective-permute-start | bytes 393224 | tf_op jit(solution)/shard_map/ppermute | solution.py:275
  58.2 20.4 %collective-permute-start.3 = (bf16[16,2,8,256]{3,2,1,0:T(8,128)(2,1)S(1)}, bf16[16,2,8,256]{3,2,1,0:T(8,128)(2,1)S(1)}, u32[]{:S(2)}, u32[]{:S(2)}) collective-permute-start(bf16[16,2,8,256]{3,2,1,0:T(8,128)(2,1)S(1)} %bitcast.95), channel_id=1, source_target_pairs={{0,128},{64,192},{128,0},{192,64},{1,129},{65,193},{129,1},{193,65... | collective-permute-start | bytes 393224 | tf_op jit(solution)/shard_map/ppermute | solution.py:275
  59.3 19.4 %collective-permute-start.4 = (bf16[16,2,8,256]{3,2,1,0:T(8,128)(2,1)S(1)}, bf16[16,2,8,256]{3,2,1,0:T(8,128)(2,1)S(1)}, u32[]{:S(2)}, u32[]{:S(2)}) collective-permute-start(bf16[16,2,8,256]{3,2,1,0:T(8,128)(2,1)S(1)} %bitcast.94), channel_id=1, source_target_pairs={{0,192},{64,0},{128,64},{192,128},{1,193},{65,1},{129,65},{193,129... | collective-permute-start | bytes 393224 | tf_op jit(solution)/shard_map/ppermute | solution.py:275
  63.4 16.5 %collective-permute-start.7 = (bf16[256,1024]{1,0:T(8,128)(2,1)S(1)}, bf16[256,1024]{1,0:T(8,128)(2,1)}, u32[]{:S(2)}, u32[]{:S(2)}) collective-permute-start(bf16[256,1024]{1,0:T(8,128)(2,1)S(1)} %bitcast.91), channel_id=1, source_target_pairs={{0,1},{1,0},{2,3},{3,2},{4,5},{5,4},{6,7},{7,6},{8,9},{9,8},{10,11... | collective-permute-start | bytes 1572872 | tf_op jit(solution)/shard_map/ppermute | solution.py:259
  66.6 13.2 %collective-permute-start.9 = (bf16[256,1024]{1,0:T(8,128)(2,1)S(1)}, bf16[256,1024]{1,0:T(8,128)(2,1)}, u32[]{:S(2)}, u32[]{:S(2)}) collective-permute-start(bf16[256,1024]{1,0:T(8,128)(2,1)S(1)} %collective-permute-done.8), channel_id=1, source_target_pairs={{0,1},{1,0},{2,3},{3,2},{4,5},{5,4},{6,7},{7,6},{8,9},{9,8},{10,11... | collective-permute-start | bytes 1572872 | tf_op jit(solution)/shard_map/ppermute | solution.py:260
  82.9 19.2 %all-to-all-start.1 = ((f32[16,64,256]{2,1,0:T(8,128)}), f32[16,64,256]{2,1,0:T(8,128)S(1)}, u32[]{:S(2)}, u32[]{:S(2)}) async-start(f32[16,64,256]{2,1,0:T(8,128)} %bitcast.87), calls=%async_computation.1 | async-start | bytes 2097152 | tf_op jit(solution)/shard_map/all_to_all | solution.py:303
  89.0 11.5 %collective-permute-start.10 = (bf16[1024,256]{1,0:T(8,128)(2,1)}, bf16[1024,256]{1,0:T(8,128)(2,1)}, u32[]{:S(2)}, u32[]{:S(2)}) collective-permute-start(bf16[1024,256]{1,0:T(8,128)(2,1)} %reshape.48), channel_id=1, source_target_pairs={{0,2},{2,0},{1,3},{3,1},{4,6},{6,4},{5,7},{7,5},{8,10},{10,8},{9,1... | collective-permute-start | bytes 1572872 | tf_op jit(solution)/shard_map/ppermute | solution.py:302
  103.0 19.6 %all-to-all-start.2 = ((f32[8,64,256]{2,1,0:T(8,128)}), f32[8,64,256]{2,1,0:T(8,128)S(1)}, u32[]{:S(2)}, u32[]{:S(2)}) async-start(f32[8,64,256]{2,1,0:T(8,128)} %broadcast_in_dim.35), calls=%async_computation.2 | async-start | bytes 1048576 | tf_op jit(solution)/shard_map/all_to_all | solution.py:308
  131.3 20.7 %collective-permute-start.16 = (f32[2,4,1,64,128]{4,3,2,1,0:T(8,128)S(1)}, f32[2,4,1,64,128]{4,3,2,1,0:T(8,128)S(1)}, u32[]{:S(2)}, u32[]{:S(2)}) collective-permute-start(f32[2,4,1,64,128]{4,3,2,1,0:T(8,128)S(1)} %bitcast_dynamic-update-slice_fusion.4), channel_id=1, source_target_pairs={{0,12},{4,0},{8,4},{12,8},{1,13},{5,1},{9,5},{13,9},{2,14},{6,2},{... | collective-permute-start | bytes 786440 | tf_op jit(solution)/shard_map/ppermute | solution.py:245
  131.5 20.4 %collective-permute-start.15 = (f32[2,4,1,64,128]{4,3,2,1,0:T(8,128)S(1)}, f32[2,4,1,64,128]{4,3,2,1,0:T(8,128)S(1)}, u32[]{:S(2)}, u32[]{:S(2)}) collective-permute-start(f32[2,4,1,64,128]{4,3,2,1,0:T(8,128)S(1)} %bitcast_dynamic-update-slice_fusion.4), channel_id=1, source_target_pairs={{0,8},{4,12},{8,0},{12,4},{1,9},{5,13},{9,1},{13,5},{2,10},{6,14},... | collective-permute-start | bytes 786440 | tf_op jit(solution)/shard_map/ppermute | solution.py:245
  135.6 9.5 %collective-permute-start.22 = (f32[2,1,4,64,128]{4,3,2,1,0:T(8,128)S(1)}, f32[2,1,4,64,128]{4,3,2,1,0:T(8,128)S(1)}, u32[]{:S(2)}, u32[]{:S(2)}) collective-permute-start(f32[2,1,4,64,128]{4,3,2,1,0:T(8,128)S(1)} %bitcast_dynamic-update-slice_fusion), channel_id=1, source_target_pairs={{0,48},{16,0},{32,16},{48,32},{1,49},{17,1},{33,17},{49,33},{2,50}... | collective-permute-start | bytes 786440 | tf_op jit(solution)/shard_map/ppermute | solution.py:245
  137.6 14.3 %collective-permute-start.14 = (f32[2,4,1,64,128]{4,3,2,1,0:T(8,128)S(1)}, f32[2,4,1,64,128]{4,3,2,1,0:T(8,128)S(1)}, u32[]{:S(2)}, u32[]{:S(2)}) collective-permute-start(f32[2,4,1,64,128]{4,3,2,1,0:T(8,128)S(1)} %bitcast_dynamic-update-slice_fusion.4), channel_id=1, source_target_pairs={{0,4},{4,8},{8,12},{12,0},{1,5},{5,9},{9,13},{13,1},{2,6},{6,10},{... | collective-permute-start | bytes 786440 | tf_op jit(solution)/shard_map/ppermute | solution.py:245
  145.1 9.2 %collective-permute-start.24 = (f32[2,1024,128]{2,1,0:T(8,128)S(1)}, f32[2,1024,128]{2,1,0:T(8,128)S(1)}, u32[]{:S(2)}, u32[]{:S(2)}) collective-permute-start(f32[2,1024,128]{2,1,0:T(8,128)S(1)} %bitcast.78), channel_id=1, source_target_pairs={{0,1},{1,0},{2,3},{3,2},{4,5},{5,4},{6,7},{7,6},{8,9},{9,8},{10,11... | collective-permute-start | bytes 3145736 | tf_op jit(solution)/shard_map/ppermute | solution.py:319
  152.2 60.2 %collective-permute-start.29 = (bf16[256,3072]{1,0:T(8,128)(2,1)}, bf16[256,3072]{1,0:T(8,128)(2,1)}, u32[]{:S(2)}, u32[]{:S(2)}) collective-permute-start(bf16[256,3072]{1,0:T(8,128)(2,1)} %bitcast.70), channel_id=1, source_target_pairs={{0,3},{1,2},{2,1},{3,0},{4,7},{5,6},{6,5},{7,4},{8,11},{9,10},{10,... | collective-permute-start | bytes 4718600 | tf_op jit(solution)/shard_map/ppermute | solution.py:251
  153.5 69.2 %collective-permute-start.28 = (bf16[256,3072]{1,0:T(8,128)(2,1)}, bf16[256,3072]{1,0:T(8,128)(2,1)}, u32[]{:S(2)}, u32[]{:S(2)}) collective-permute-start(bf16[256,3072]{1,0:T(8,128)(2,1)} %bitcast.70), channel_id=1, source_target_pairs={{0,2},{1,3},{2,0},{3,1},{4,6},{5,7},{6,4},{7,5},{8,10},{9,11},{10,... | collective-permute-start | bytes 4718600 | tf_op jit(solution)/shard_map/ppermute | solution.py:251
  154.0 68.7 %collective-permute-start.27 = (bf16[256,3072]{1,0:T(8,128)(2,1)}, bf16[256,3072]{1,0:T(8,128)(2,1)}, u32[]{:S(2)}, u32[]{:S(2)}) collective-permute-start(bf16[256,3072]{1,0:T(8,128)(2,1)} %bitcast.70), channel_id=1, source_target_pairs={{0,1},{1,0},{2,3},{3,2},{4,5},{5,4},{6,7},{7,6},{8,9},{9,8},{10,11... | collective-permute-start | bytes 4718600 | tf_op jit(solution)/shard_map/ppermute | solution.py:251
  154.4 54.8 %collective-permute-start.25 = (bf16[1024,256]{1,0:T(8,128)(2,1)}, bf16[1024,256]{1,0:T(8,128)(2,1)}, u32[]{:S(2)}, u32[]{:S(2)}) collective-permute-start(bf16[1024,256]{1,0:T(8,128)(2,1)} %reshape.48), channel_id=1, source_target_pairs={{0,1},{1,0},{2,3},{3,2},{4,5},{5,4},{6,7},{7,6},{8,9},{9,8},{10,11... | collective-permute-start | bytes 1572872 | tf_op jit(solution)/shard_map/ppermute | solution.py:259
  156.7 52.5 %collective-permute-start.26 = (bf16[1024,256]{1,0:T(8,128)(2,1)}, bf16[1024,256]{1,0:T(8,128)(2,1)}, u32[]{:S(2)}, u32[]{:S(2)}) collective-permute-start(bf16[1024,256]{1,0:T(8,128)(2,1)} %collective-permute-done.10), channel_id=1, source_target_pairs={{0,1},{1,0},{2,3},{3,2},{4,5},{5,4},{6,7},{7,6},{8,9},{9,8},{10,11... | collective-permute-start | bytes 1572872 | tf_op jit(solution)/shard_map/ppermute | solution.py:260
  (14 other events, 78.9 us)
